TPU v7x, 256 devices: a whole 4x4x8 slice. The times are simulated.
256 devices in a mesh: sector: 32 (over x, z_lo, core), layer: 8 (over y, z_hi).
Axes of the slice: x: 4, y: 4, z: 8 (z_hi: 2, z_lo: 4; z = z_hi * 4 + z_lo), core: 2. Of those that a mesh axis runs over, the one named last changes fastest.
Arguments:
- rotor_state: float32 [5, 8, 128, 16384], P(None, None, 'layer', 'sector'), may hold values from -1.5 to 4, as said below
- cavity_state: float32 [5, 4, 128, 16384], P(None, None, 'layer', 'sector'), may hold values from -1.5 to 4, as said below
- block_map: int32 [32], replicated, may hold values from 0 to 31, each once
- rotor_offset: int32 [1], replicated, may hold values from 0 to 511
Outputs:
- rotor_next: float32 [5, 8, 128, 16384], P(None, None, 'layer', 'sector')
- cavity_next: float32 [5, 4, 128, 16384], P(None, None, 'layer', 'sector')
Inputs may be any that keep to these rules, and one draw needn't show every extreme that they name: `rotor_state`: component 0 lies in 0.5 to 1.5, components 1 to 3 in -1.5 to 1.5, component 4 in 2 to 4. `cavity_state`: component 0 lies in 0.5 to 1.5, components 1 to 3 in -1.5 to 1.5, component 4 in 2 to 4. `block_map`: each of 0 to 31 once.
All inputs are finite; a program needn't handle non-finite values.
Results may differ from a plain program's by a relative error of at most 0.00002.
Values sent between devices are 32-bit elements; how exact they have to be, the bound alone decides.
A program may use at most 192 MiB of HBM per device.

v0:
```python
import jax
import jax.numpy as jnp
from jax import lax
from jax.sharding import PartitionSpec as P

DIFFUSION = 0.05
COURANT = 0.1


def with_halo(cells, sides, width, closed):
    for axis, dim in sides:
        count = lax.axis_size(axis)
        ends = count if closed else count - 1
        head = lax.slice_in_dim(cells, 0, width, axis=dim)
        tail = lax.slice_in_dim(cells, cells.shape[dim] - width, cells.shape[dim], axis=dim)
        cells = jnp.concatenate(
            [
                lax.ppermute(tail, axis, [(i, (i + 1) % count) for i in range(ends)]),
                cells,
                lax.ppermute(head, axis, [((i + 1) % count, i) for i in range(ends)]),
            ],
            axis=dim,
        )
    return cells


def shifted(value, axis, steps):
    count = lax.axis_size(axis)
    pairs = [(source, (source + steps) % count) for source in range(count)]
    return lax.ppermute(value, axis, pairs)


def viscosity(density, energy):
    return 0.5 * (energy / density) ** 0.7


def region_update(region, seam_ghost, seam_last):
    cycle_padded = with_halo(region, (("sector", 3),), 1, True)
    radial_padded = with_halo(region, (("layer", 2),), 1, False)
    layer_here = lax.axis_index("layer")
    layers = lax.axis_size("layer")
    radial_rows = region.shape[2]
    viscous = viscosity(region[0], region[4])
    ghost_viscous = viscosity(seam_ghost[0], seam_ghost[4])
    if seam_last:
        extended = jnp.concatenate([region, seam_ghost[:, None]], axis=1)
        extended_mu = jnp.concatenate([viscous, ghost_viscous[None]], axis=0)
    else:
        extended = jnp.concatenate([seam_ghost[:, None], region], axis=1)
        extended_mu = jnp.concatenate([ghost_viscous[None], viscous], axis=0)
    face_axial = (
        0.5
        * (extended_mu[None, 1:] + extended_mu[None, :-1])
        * (extended[:, 1:] - extended[:, :-1])
    )
    empty_plane = jnp.zeros_like(face_axial[:, :1])
    if seam_last:
        axial_sum = face_axial - jnp.concatenate([empty_plane, face_axial[:, :-1]], axis=1)
    else:
        axial_sum = jnp.concatenate([face_axial[:, 1:], empty_plane], axis=1) - face_axial
    radial_mu = viscosity(radial_padded[0], radial_padded[4])
    face_radial = (
        0.5
        * (radial_mu[None, :, 1:] + radial_mu[None, :, :-1])
        * (radial_padded[:, :, 1:] - radial_padded[:, :, :-1])
    )
    face_index = jnp.arange(radial_rows + 1, dtype=jnp.int32)
    closed = (face_index == 0) & (layer_here == 0) | (face_index == radial_rows) & (
        layer_here == layers - 1
    )
    face_radial = jnp.where(closed[None, None, :, None], 0.0, face_radial)
    radial = face_radial[:, :, 1:] - face_radial[:, :, :-1]
    cycle_mu = viscosity(cycle_padded[0], cycle_padded[4])
    face_cycle = (
        0.5
        * (cycle_mu[None, ..., 1:] + cycle_mu[None, ..., :-1])
        * (cycle_padded[..., 1:] - cycle_padded[..., :-1])
    )
    cycle_sum = face_cycle[..., 1:] - face_cycle[..., :-1]
    velocity = cycle_padded[3] / cycle_padded[0]
    carried = velocity[None] * cycle_padded
    advected = -COURANT * 0.5 * (carried[..., 2:] - carried[..., :-2])
    return region + DIFFUSION * (axial_sum + radial + cycle_sum) + advected


def shards(rotor_state, cavity_state, block_map, rotor_offset):
    sectors = lax.axis_size("sector")
    position = lax.axis_index("sector")
    components = rotor_state.shape[0]
    radial_rows = rotor_state.shape[2]
    cycle_cells = rotor_state.shape[3]
    block_cells = cycle_cells // sectors
    offset_cells = rotor_offset[0]
    slot_index = jnp.arange(sectors, dtype=jnp.int32)
    rotor_seam = rotor_state[:, -1].reshape(components, radial_rows, sectors, block_cells)
    cavity_seam = cavity_state[:, 0]
    following = shifted(cavity_seam, "sector", -1)
    lifted = lax.dynamic_slice_in_dim(
        jnp.concatenate([cavity_seam, following], axis=2), offset_cells, cycle_cells, axis=2
    )
    lifted = lifted.reshape(components, radial_rows, sectors, block_cells)
    every_rotor = lax.all_gather(rotor_seam, "sector", axis=2, tiled=True)
    landed = jnp.take(every_rotor, (position - block_map) % sectors * sectors + slot_index, axis=2)
    every_cavity = lax.all_gather(lifted, "sector", axis=2, tiled=True)
    returned = jnp.take(
        every_cavity, (position + block_map) % sectors * sectors + slot_index, axis=2
    )
    landed_flat = landed.reshape(components, radial_rows, cycle_cells)
    preceding = shifted(landed_flat, "sector", 1)
    cavity_ghost = lax.dynamic_slice_in_dim(
        jnp.concatenate([preceding, landed_flat], axis=2),
        cycle_cells - offset_cells,
        cycle_cells,
        axis=2,
    )
    rotor_ghost = returned.reshape(components, radial_rows, cycle_cells)
    rotor_next = region_update(rotor_state, rotor_ghost, True)
    cavity_next = region_update(cavity_state, cavity_ghost, False)
    return (rotor_next, cavity_next)


def solution(mesh):
    placed = (P(None, None, "layer", "sector"), P(None, None, "layer", "sector"), P(), P())
    return jax.shard_map(
        shards,
        mesh=mesh,
        in_specs=placed,
        out_specs=(P(None, None, "layer", "sector"), P(None, None, "layer", "sector")),
        check_vma=False,
    )
```

profile of v0, /device:TPU:8, one launch (start us, length us, event | category | flops | bytes accessed | tf_op | source)
XLA Modules:
  0.0 518.3 jit_solution(2654275196244347219)
XLA Ops:
  8.6 1.8 copy.22
  10.5 1.0 copy-done.1
  11.5 6.3 %collective-permute-start = (f32[5,16,512]{2,1,0:T(8,128)S(1)}, f32[5,16,512]{2,1,0:T(8,128)S(1)}, u32[]{:S(2)}, u32[]{:S(2)}) collective-permute-start(f32[5,16,512]{2,1,0:T(8,128)S(1)} %slice_bitcast_fusion), channel_id=1, source_target_pairs={{0,248},{8,0},{16,8},{24,16},{32,24},{40,32},{48,40},{56,48},{64,5... | collective-permute-start | bytes 491528 | tf_op jit(solution)/shard_map/ppermute | solution.py:30
  18.5 3.2 collective-permute-done
  22.3 1.8 copy.12
  24.4 5.9 %collective-permute-start.9 = (f32[5,4,16,1]{3,2,1,0:T(8,128)S(1)}, f32[5,4,16,1]{3,2,1,0:T(8,128)S(1)}, u32[]{:S(2)}, u32[]{:S(2)}) collective-permute-start(f32[5,4,16,1]{3,2,1,0:T(8,128)S(1)} %get-tuple-element.18), channel_id=1, source_target_pairs={{8,0},{16,8},{24,16},{32,24},{40,32},{48,40},{56,48},{64,56},{72,6... | collective-permute-start | bytes 3848 | tf_op jit(solution)/shard_map/ppermute | solution.py:20
  31.0 5.4 %collective-permute-start.6 = (f32[5,4,1,512]{3,2,1,0:T(1,128)}, f32[5,4,1,512]{3,2,1,0:T(1,128)S(1)}, u32[]{:S(2)}, u32[]{:S(2)}) collective-permute-start(f32[5,4,1,512]{3,2,1,0:T(1,128)} %get-tuple-element.15), channel_id=1, source_target_pairs={{0,1},{1,2},{2,3},{3,4},{4,5},{5,6},{6,7},{8,9},{9,10},{10,11},{11... | collective-permute-start | bytes 122888 | tf_op jit(solution)/shard_map/ppermute | solution.py:18
  36.4 5.2 %collective-permute-start.7 = (f32[5,4,1,512]{3,2,1,0:T(1,128)}, f32[5,4,1,512]{3,2,1,0:T(1,128)S(1)}, u32[]{:S(2)}, u32[]{:S(2)}) collective-permute-start(f32[5,4,1,512]{3,2,1,0:T(1,128)} %get-tuple-element.16), channel_id=1, source_target_pairs={{1,0},{2,1},{3,2},{4,3},{5,4},{6,5},{7,6},{9,8},{10,9},{11,10},{12... | collective-permute-start | bytes 122888 | tf_op jit(solution)/shard_map/ppermute | solution.py:20
  45.7 5.6 %collective-permute-start.4 = (f32[5,8,16,1]{3,2,1,0:T(8,128)}, f32[5,8,16,1]{3,2,1,0:T(8,128)S(1)}, u32[]{:S(2)}, u32[]{:S(2)}) collective-permute-start(f32[5,8,16,1]{3,2,1,0:T(8,128)} %get-tuple-element.12), channel_id=1, source_target_pairs={{8,0},{16,8},{24,16},{32,24},{40,32},{48,40},{56,48},{64,56},{72,6... | collective-permute-start | bytes 7688 | tf_op jit(solution)/shard_map/ppermute | solution.py:20
  51.4 4.5 collective-permute-start.1
  56.7 1.3 broadcast_multiply_fusion.1
  58.0 8.8 %collective-permute-done.3 = f32[5,8,16,1]{3,2,1,0:T(8,128)S(1)} collective-permute-done((f32[5,8,16,1]{3,2,1,0:T(8,128)}, f32[5,8,16,1]{3,2,1,0:T(8,128)S(1)}, u32[]{:S(2)}, u32[]{:S(2)}) %collective-permute-start.3) | collective-permute-done | bytes 2592 | tf_op jit(solution)/shard_map/ppermute | solution.py:18
  66.8 3.3 collective-permute-start.2
  71.1 1.7 fusion.2
  72.8 1.8 broadcast_multiply_fusion
  74.8 1.2 fusion.12
  76.1 2.9 collective-permute-done.2
  79.5 1.8 fusion.1
  81.3 177.8 %all-gather.5.cloned.1.call-done = f32[5,16,1024,16]{3,1,2,0:T(8,128)} async-done(((f32[5,16,32,16]{3,1,2,0:T(8,128)}), f32[5,16,1024,16]{3,1,2,0:T(8,128)}) %all-gather.5.cloned.1.call-update) | async-done | bytes 5242896 | tf_op jit(solution)/shard_map/all_gather | solution.py:102
  259.0 3.0 gather_fusion.1
  262.0 225.4 %all-gather.3.cloned.1.call-done = f32[5,16,1024,16]{3,1,2,0:T(8,128)} async-done(((f32[5,16,32,16]{3,1,2,0:T(8,128)}), f32[5,16,1024,16]{3,1,2,0:T(8,128)}) %all-gather.3.cloned.1.call-update) | async-done | bytes 5242896 | tf_op jit(solution)/shard_map/all_gather | solution.py:104
  487.4 3.0 gather_fusion
  490.4 1.9 select_bitcast_fusion
  492.4 1.5 copy.14
  494.0 1.5 copy.23
  495.5 2.8 reshape.106
  498.6 2.1 broadcast_in_dim_reshape.3
  501.5 1.1 mul.216
  503.1 1.0 copy-done.3
  505.2 2.1 fusion.4
  507.4 1.1 fusion.41
  510.0 1.4 fusion.15
  (73 shorter events, 13.9 us)
Async XLA Ops:
  7.2 251.9 %all-gather.5.cloned.1.call-start = ((), (), s32[]{:S(2)}) async-start(), calls=%async_computation.1 | async-start | bytes 43253760 | tf_op jit(solution)/shard_map/all_gather | solution.py:102
  10.4 1.1 copy-start.1
  10.4 477.0 %all-gather.3.cloned.1.call-start = ((), (), s32[]{:S(2)}) async-start(), calls=%async_computation | async-start | bytes 43253760 | tf_op jit(solution)/shard_map/all_gather | solution.py:104
  11.5 10.2 %collective-permute-start = (f32[5,16,512]{2,1,0:T(8,128)S(1)}, f32[5,16,512]{2,1,0:T(8,128)S(1)}, u32[]{:S(2)}, u32[]{:S(2)}) collective-permute-start(f32[5,16,512]{2,1,0:T(8,128)S(1)} %slice_bitcast_fusion), channel_id=1, source_target_pairs={{0,248},{8,0},{16,8},{24,16},{32,24},{40,32},{48,40},{56,48},{64,5... | collective-permute-start | bytes 491528 | tf_op jit(solution)/shard_map/ppermute | solution.py:30
  24.1 17.5 %copy-start = (f32[5,8,16,512]{3,2,1,0:T(8,128)S(1)}, f32[5,8,16,512]{3,2,1,0:T(8,128)}, u32[]{:S(2)}) copy-start(f32[5,8,16,512]{3,2,1,0:T(8,128)} %param.6) | copy-start | bytes 3932164
  24.2 18.4 %copy-start.10 = (s32[32]{0:T(128)S(1)}, s32[32]{0:T(128)}, u32[]{:S(2)}) copy-start(s32[32]{0:T(128)} %param.8) | copy-start | bytes 388
  24.3 21.4 %collective-permute-start.8 = (f32[5,4,16,1]{3,2,1,0:T(8,128)S(1)}, f32[5,4,16,1]{3,2,1,0:T(8,128)S(1)}, u32[]{:S(2)}, u32[]{:S(2)}) collective-permute-start(f32[5,4,16,1]{3,2,1,0:T(8,128)S(1)} %get-tuple-element.17), channel_id=1, source_target_pairs={{0,8},{8,16},{16,24},{24,32},{32,40},{40,48},{48,56},{56,64},{64,7... | collective-permute-start | bytes 3848 | tf_op jit(solution)/shard_map/ppermute | solution.py:18
  24.4 27.0 %collective-permute-start.9 = (f32[5,4,16,1]{3,2,1,0:T(8,128)S(1)}, f32[5,4,16,1]{3,2,1,0:T(8,128)S(1)}, u32[]{:S(2)}, u32[]{:S(2)}) collective-permute-start(f32[5,4,16,1]{3,2,1,0:T(8,128)S(1)} %get-tuple-element.18), channel_id=1, source_target_pairs={{8,0},{16,8},{24,16},{32,24},{40,32},{48,40},{56,48},{64,56},{72,6... | collective-permute-start | bytes 3848 | tf_op jit(solution)/shard_map/ppermute | solution.py:20
  31.0 43.6 %collective-permute-start.6 = (f32[5,4,1,512]{3,2,1,0:T(1,128)}, f32[5,4,1,512]{3,2,1,0:T(1,128)S(1)}, u32[]{:S(2)}, u32[]{:S(2)}) collective-permute-start(f32[5,4,1,512]{3,2,1,0:T(1,128)} %get-tuple-element.15), channel_id=1, source_target_pairs={{0,1},{1,2},{2,3},{3,4},{4,5},{5,6},{6,7},{8,9},{9,10},{10,11},{11... | collective-permute-start | bytes 122888 | tf_op jit(solution)/shard_map/ppermute | solution.py:18
  36.4 38.2 %collective-permute-start.7 = (f32[5,4,1,512]{3,2,1,0:T(1,128)}, f32[5,4,1,512]{3,2,1,0:T(1,128)S(1)}, u32[]{:S(2)}, u32[]{:S(2)}) collective-permute-start(f32[5,4,1,512]{3,2,1,0:T(1,128)} %get-tuple-element.16), channel_id=1, source_target_pairs={{1,0},{2,1},{3,2},{4,3},{5,4},{6,5},{7,6},{9,8},{10,9},{11,10},{12... | collective-permute-start | bytes 122888 | tf_op jit(solution)/shard_map/ppermute | solution.py:20
  42.6 24.3 %collective-permute-start.3 = (f32[5,8,16,1]{3,2,1,0:T(8,128)}, f32[5,8,16,1]{3,2,1,0:T(8,128)S(1)}, u32[]{:S(2)}, u32[]{:S(2)}) collective-permute-start(f32[5,8,16,1]{3,2,1,0:T(8,128)} %get-tuple-element.11), channel_id=1, source_target_pairs={{0,8},{8,16},{16,24},{24,32},{32,40},{40,48},{48,56},{56,64},{64,7... | collective-permute-start | bytes 7688 | tf_op jit(solution)/shard_map/ppermute | solution.py:18
  45.7 24.4 %collective-permute-start.4 = (f32[5,8,16,1]{3,2,1,0:T(8,128)}, f32[5,8,16,1]{3,2,1,0:T(8,128)S(1)}, u32[]{:S(2)}, u32[]{:S(2)}) collective-permute-start(f32[5,8,16,1]{3,2,1,0:T(8,128)} %get-tuple-element.12), channel_id=1, source_target_pairs={{8,0},{16,8},{24,16},{32,24},{40,32},{48,40},{56,48},{64,56},{72,6... | collective-permute-start | bytes 7688 | tf_op jit(solution)/shard_map/ppermute | solution.py:20
  51.4 24.6 %collective-permute-start.1 = (f32[5,8,1,512]{3,1,2,0:T(8,128)}, f32[5,8,1,512]{3,1,2,0:T(8,128)S(1)}, u32[]{:S(2)}, u32[]{:S(2)}) collective-permute-start(f32[5,8,1,512]{3,1,2,0:T(8,128)} %copy.24), channel_id=1, source_target_pairs={{0,1},{1,2},{2,3},{3,4},{4,5},{5,6},{6,7},{8,9},{9,10},{10,11},{11... | collective-permute-start | bytes 245768 | tf_op jit(solution)/shard_map/ppermute | solution.py:18
  56.7 10.1 %copy-start.9 = (f32[5,8,1,512]{3,1,2,0:T(8,128)S(1)}, f32[5,8,1,512]{3,1,2,0:T(8,128)}, u32[]{:S(2)}) copy-start(f32[5,8,1,512]{3,1,2,0:T(8,128)} %copy.25) | copy-start | bytes 245764
  66.8 12.1 %collective-permute-start.2 = (f32[5,8,1,512]{3,1,2,0:T(8,128)S(1)}, f32[5,8,1,512]{3,1,2,0:T(8,128)S(1)}, u32[]{:S(2)}, u32[]{:S(2)}) collective-permute-start(f32[5,8,1,512]{3,1,2,0:T(8,128)S(1)} %copy-done.9), channel_id=1, source_target_pairs={{1,0},{2,1},{3,2},{4,3},{5,4},{6,5},{7,6},{9,8},{10,9},{11,10},{12... | collective-permute-start | bytes 245768 | tf_op jit(solution)/shard_map/ppermute | solution.py:20
  498.3 4.3 copy-start.7
  498.3 9.0 %collective-permute-start.5 = (f32[5,16,512]{2,1,0:T(8,128)}, f32[5,16,512]{2,1,0:T(8,128)}, u32[]{:S(2)}, u32[]{:S(2)}) collective-permute-start(f32[5,16,512]{2,1,0:T(8,128)} %reshape.106), channel_id=1, source_target_pairs={{0,8},{8,16},{16,24},{24,32},{32,40},{40,48},{48,56},{56,64},{64,7... | collective-permute-start | bytes 491528 | tf_op jit(solution)/shard_map/ppermute | solution.py:30
  502.6 1.4 copy-start.3
  502.7 2.0 copy-start.4
  502.9 2.3 copy-start.2
  505.2 3.3 copy-start.8
  508.5 1.1 copy-start.5
  508.5 1.4 copy-start.6
Sparse Core Ops, SparseCore 0:
  10.6 248.4 all-gather.4
  260.9 226.4 all-gather.2
where the time goes:
time: 521 us; the launch traced here: 518 us
  waiting for transfers between devices  418 us (80%)
  starting transfers between devices  36.7 us (7%)
  local copies, waits for them, and re-layouts  29.2 us (6%)
  other arithmetic  19.2 us (4%)
  between operations  15.1 us (3%)
    all_gather x1, waiting for transfers between devices, shards(): every_cavity = lax.all_gather(lifted, 'sector', axis=2, tiled=True)  225 us
    all_gather x1, waiting for transfers between devices, shards(): every_rotor = lax.all_gather(rotor_seam, 'sector', axis=2, tiled=True)  178 us
    ppermute x4, starting transfers between devices, with_halo(): lax.ppermute(head, axis, [((i + 1) % count, i) for i in range(ends)])  20.1 us
  transfers between devices with their start and end apart: 12, of which 5 were waited for; matrix products, arithmetic and copies ran while one was open for 5% of the time, Pallas kernels for 0%

commit v1 on v0

v1 whole, which is shorter than its diff:
```python
import functools

import jax
import jax.numpy as jnp
from jax import lax
from jax.experimental import pallas as pl
from jax.experimental.pallas import tpu as pltpu
from jax.sharding import PartitionSpec as P

DIFFUSION = 0.05
LANES = 128
SUB = 8
MESH = pl.DeviceIdType.MESH


def viscosity(density, energy):
    return 0.5 * jnp.exp(0.7 * jnp.log(energy / density))


def iota(axis):
    return lax.broadcasted_iota(jnp.int32, (SUB, LANES), axis)


def granule_transpose(x):
    sub, granule = iota(0), iota(1) // 16
    for bit in range(3):
        s, g = 1 << bit, 16 << bit
        a = (sub // s) % 2
        b = (granule // s) % 2
        up = pltpu.roll(pltpu.roll(x, g, axis=1), SUB - s, axis=0)
        down = pltpu.roll(pltpu.roll(x, LANES - g, axis=1), s, axis=0)
        x = jnp.where(a == b, x, jnp.where(b == 1, up, down))
    return x


def kernel(
    map_ref, offset_ref, rotor_hbm, cavity_hbm, rotor_out, cavity_out,
    rotor, cavity, rotor_new, cavity_new, mu_r, mu_c, w_r, w_c,
    two_cavity, two_landed, rotor_ghost, cavity_ghost,
    packed, send_r, recv_r, send_c, recv_c,
    low_own, high_own, low_got, high_got, col_own, col_got, inverse,
    load_sem, store_sem, send_r_sem, recv_r_sem, send_c_sem, recv_c_sem, shift_send, shift_recv, edge_send, edge_recv,
):
    sectors = lax.axis_size("sector")
    layers = lax.axis_size("layer")
    me = lax.axis_index("sector")
    layer = lax.axis_index("layer")
    comps, tiles, rows_r, _ = rotor.shape
    rows_c = cavity.shape[2]
    rows = two_cavity.shape[2]
    width = tiles * LANES
    planes_r, planes_c = rows_r // rows, rows_c // rows
    last_r = rows_r - rows
    used = comps * 2

    def sector_at(step):
        return {"sector": lax.rem(me + step + sectors, sectors)}

    loads = []
    for t in range(tiles):
        loads.append(pltpu.make_async_copy(
            rotor_hbm.at[:, pl.ds(last_r, rows), pl.ds(t * LANES, LANES)], two_landed.at[t], load_sem.at[t]))
    for t in range(tiles):
        loads.append(pltpu.make_async_copy(
            cavity_hbm.at[:, pl.ds(0, rows), pl.ds(t * LANES, LANES)], two_cavity.at[t], load_sem.at[tiles + t]))
    for hbm, region, base in ((rotor_hbm, rotor, 2 * tiles), (cavity_hbm, cavity, 3 * tiles)):
        for t in range(tiles):
            loads.append(pltpu.make_async_copy(
                hbm.at[:, :, pl.ds(t * LANES, LANES)], region.at[:, t], load_sem.at[base + t]))
    for copy in loads:
        copy.start()

    barrier = pltpu.get_barrier_semaphore()

    def greet(k, carry):
        pl.semaphore_signal(barrier, inc=1, device_id=sector_at(k), device_id_type=MESH)
        return carry

    lax.fori_loop(1, sectors, greet, 0)

    @pl.when(layer > 0)
    def _():
        pl.semaphore_signal(barrier, inc=1, device_id={"layer": layer - 1}, device_id_type=MESH)

    @pl.when(layer < layers - 1)
    def _():
        pl.semaphore_signal(barrier, inc=1, device_id={"layer": layer + 1}, device_id_type=MESH)

    def invert(k, carry):
        found = jnp.int32(0)
        for j in range(sectors):
            found = jnp.where(map_ref[j] == k, jnp.int32(j), found)
        inverse[k] = found
        return carry

    lax.fori_loop(0, sectors, invert, 0)

    def pack(source, base, send, recv):
        def one(t, carry):
            for q in range(used):
                tile = source[base + t, q // 2, pl.ds(SUB * (q % 2), SUB), :]
                packed[pl.ds(SUB * t, SUB), q, :] = granule_transpose(tile)
            return carry

        lax.fori_loop(0, tiles, one, 0)
        recv[0] = packed[inverse[0]]

        def slot(k, carry):
            send[k] = packed[inverse[k]]
            return carry

        lax.fori_loop(1, sectors, slot, 0)

    def unpack(recv, target, base):
        def block(j, carry):
            packed[j] = recv[map_ref[j]]
            return carry

        lax.fori_loop(0, sectors, block, 0)

        def one(t, carry):
            for q in range(used):
                tile = packed[pl.ds(SUB * t, SUB), q, :]
                target[base + t, q // 2, pl.ds(SUB * (q % 2), SUB), :] = granule_transpose(tile)
            return carry

        lax.fori_loop(0, tiles, one, 0)

    def block_copy(send, recv, send_sem, recv_sem, k, sign):
        return pltpu.make_async_remote_copy(
            src_ref=send.at[k, pl.ds(0, used)], dst_ref=recv.at[k, pl.ds(0, used)],
            send_sem=send_sem.at[k], recv_sem=recv_sem.at[k],
            device_id=sector_at(sign * k), device_id_type=MESH)

    def start_blocks(send, recv, send_sem, recv_sem, sign):
        def one(k, carry):
            block_copy(send, recv, send_sem, recv_sem, k, sign).start()
            return carry

        lax.fori_loop(1, sectors, one, 0)

    def wait_blocks(send, recv, send_sem, recv_sem, sign, arrived):
        def one(k, carry):
            copy = block_copy(send, recv, send_sem, recv_sem, k, sign)
            if arrived:
                copy.wait_recv()
            else:
                copy.wait_send()
            return carry

        lax.fori_loop(1, sectors, one, 0)

    def shift_copy(buffer, source, target, index, step):
        return pltpu.make_async_remote_copy(
            src_ref=buffer.at[pl.ds(source, tiles)], dst_ref=buffer.at[pl.ds(target, tiles)],
            send_sem=shift_send.at[index], recv_sem=shift_recv.at[index],
            device_id=sector_at(step), device_id_type=MESH)

    def shifted(buffer, target, start):
        tile0 = lax.div(start, jnp.int32(LANES))
        rest = lax.rem(start, jnp.int32(LANES))
        back = lax.rem(LANES - rest, jnp.int32(LANES))
        keep = lax.broadcasted_iota(jnp.int32, (rows, LANES), 1) < LANES - rest
        for t in range(tiles):
            i0 = tile0 + t
            i1 = jnp.minimum(i0 + 1, 2 * tiles - 1)
            for c in range(comps):
                here = pltpu.roll(buffer[i0, c], back, axis=1)
                after = pltpu.roll(buffer[i1, c], back, axis=1)
                target[t, c] = jnp.where(keep, here, after)

    offset = offset_ref[0]

    for t in range(tiles):
        loads[t].wait()
    pack(two_landed, 0, send_r, recv_r)
    for t in range(tiles):
        loads[tiles + t].wait()

    pl.semaphore_wait(barrier, sectors - 1 + jnp.where(layer > 0, 1, 0) + jnp.where(layer < layers - 1, 1, 0))

    cavity_shift = shift_copy(two_cavity, 0, tiles, 0, -1)
    cavity_shift.start()
    start_blocks(send_r, recv_r, send_r_sem, recv_r_sem, 1)

    for copy in loads[2 * tiles:]:
        copy.wait()

    first_c = comps * tiles * planes_r
    for edge, own in ((0, low_own), (rows - 1, high_own)):
        for c in range(comps):
            for t in range(tiles):
                own[pl.ds((c * tiles + t) * planes_r, planes_r), :] = rotor[c, t, pl.ds(edge, planes_r, stride=rows), :]
                own[pl.ds(first_c + (c * tiles + t) * planes_c, planes_c), :] = cavity[
                    c, t, pl.ds(edge, planes_c, stride=rows), :]

    up_copy = pltpu.make_async_remote_copy(
        src_ref=high_own, dst_ref=low_got, send_sem=edge_send.at[0], recv_sem=edge_recv.at[0],
        device_id={"layer": lax.rem(layer + 1, layers)}, device_id_type=MESH)
    down_copy = pltpu.make_async_remote_copy(
        src_ref=low_own, dst_ref=high_got, send_sem=edge_send.at[1], recv_sem=edge_recv.at[1],
        device_id={"layer": lax.rem(layer + layers - 1, layers)}, device_id_type=MESH)

    @pl.when(layer < layers - 1)
    def _():
        up_copy.start()

    @pl.when(layer > 0)
    def _():
        down_copy.start()

    lane = iota(1)
    pieces = []
    for c in range(comps):
        for region, new, planes in ((rotor, rotor_new, planes_r), (cavity, cavity_new, planes_c)):
            for p in range(planes):
                for half in range(2):
                    pieces.append((region, new, c, p * rows + half * SUB))
    group = len(pieces) // comps
    zero = jnp.zeros((SUB, LANES), jnp.float32)
    head, tail = zero, zero
    for v, (region, _, c, r) in enumerate(pieces):
        head = jnp.where(lane == v, region[c, 0, pl.ds(r, SUB), :][:, 0:1], head)
        tail = jnp.where(lane == v, region[c, tiles - 1, pl.ds(r, SUB), :][:, LANES - 1:], tail)
    col_own[0] = head
    col_own[1] = tail
    col_copies = [
        pltpu.make_async_remote_copy(
            src_ref=col_own.at[i], dst_ref=col_got.at[i], send_sem=edge_send.at[2 + i], recv_sem=edge_recv.at[2 + i],
            device_id=sector_at(-1 if i == 0 else 1), device_id_type=MESH)
        for i in range(2)
    ]
    for copy in col_copies:
        copy.start()

    rate = jnp.float32(DIFFUSION)
    half_rate = jnp.float32(0.5 * DIFFUSION)
    wide_lane = lax.broadcasted_iota(jnp.int32, (rows, width), 1)
    wide_row = lax.broadcasted_iota(jnp.int32, (rows, width), 0)

    def whole(region, c, at):
        return jnp.concatenate([region[c, t, at, :] for t in range(tiles)], axis=1)

    def interior(region, new, mu, w, planes):
        def first(p, carry):
            at = pl.ds(pl.multiple_of(p * rows, rows), rows)
            density = whole(region, 0, at)
            mu[p] = viscosity(density, whole(region, 4, at))
            w[p] = whole(region, 3, at) / density
            return carry

        lax.fori_loop(0, planes, first, 0)

        def one(p, carry):
            at = pl.ds(pl.multiple_of(p * rows, rows), rows)
            above = jnp.minimum(p + 1, planes - 1)
            below = jnp.maximum(p - 1, 0)
            at_above = pl.ds(pl.multiple_of(above * rows, rows), rows)
            at_below = pl.ds(pl.multiple_of(below * rows, rows), rows)
            m = mu[p]
            up = half_rate * (m + mu[above])
            down = half_rate * (m + mu[below])
            radial = jnp.where(wide_row == rows - 1, 0.0, half_rate * (m + pltpu.roll(m, rows - 1, axis=0)))
            cycle = half_rate * (m + pltpu.roll(m, width - 1, axis=1))
            speed = rate * w[p]
            ahead = pltpu.roll(speed, width - 1, axis=1)
            inner = wide_lane < width - 1
            next_factor = jnp.where(inner, cycle - ahead, 0.0)
            here_factor = jnp.where(inner, cycle + speed, 0.0)
            for c in range(comps):
                q = whole(region, c, at)
                total = q + up * (whole(region, c, at_above) - q) + down * (whole(region, c, at_below) - q)
                face = radial * (pltpu.roll(q, rows - 1, axis=0) - q)
                total = total + (face - pltpu.roll(face, 1, axis=0))
                face = next_factor * pltpu.roll(q, width - 1, axis=1) - here_factor * q
                total = total + (face - pltpu.roll(face, 1, axis=1))
                for t in range(tiles):
                    new[c, t, at, :] = total[:, t * LANES:(t + 1) * LANES]
            return carry

        lax.fori_loop(0, planes, one, 0)

    interior(rotor, rotor_new, mu_r, w_r, planes_r)
    interior(cavity, cavity_new, mu_c, w_c, planes_c)

    cavity_shift.wait_recv()
    shifted(two_cavity, rotor_ghost, offset)
    pack(rotor_ghost, 0, send_c, recv_c)
    start_blocks(send_c, recv_c, send_c_sem, recv_c_sem, -1)

    wait_blocks(send_r, recv_r, send_r_sem, recv_r_sem, 1, True)
    unpack(recv_r, two_landed, tiles)
    landed_shift = shift_copy(two_landed, tiles, 0, 1, 1)
    landed_shift.start()

    def edge_fix(own, got, edge):
        for region, new, planes, base in ((rotor, rotor_new, planes_r, 0), (cavity, cavity_new, planes_c, first_c)):
            size = tiles * planes
            a = [own[pl.ds(base + c * size, size), :] for c in range(comps)]
            b = [got[pl.ds(base + c * size, size), :] for c in range(comps)]
            factor = half_rate * (viscosity(a[0], a[4]) + viscosity(b[0], b[4]))
            for c in range(comps):
                change = factor * (b[c] - a[c])
                for t in range(tiles):
                    at = (c, t, pl.ds(edge, planes, stride=rows), slice(None))
                    new[at] = new[at] + change[t * planes:(t + 1) * planes]

    @pl.when(layer < layers - 1)
    def _():
        down_like = pltpu.make_async_remote_copy(
            src_ref=low_own, dst_ref=high_got, send_sem=edge_send.at[1], recv_sem=edge_recv.at[1],
            device_id={"layer": lax.rem(layer + 1, layers)}, device_id_type=MESH)
        down_like.wait_recv()
        edge_fix(high_own, high_got, rows - 1)

    @pl.when(layer > 0)
    def _():
        up_like = pltpu.make_async_remote_copy(
            src_ref=high_own, dst_ref=low_got, send_sem=edge_send.at[0], recv_sem=edge_recv.at[0],
            device_id={"layer": lax.rem(layer + layers - 1, layers)}, device_id_type=MESH)
        up_like.wait_recv()
        edge_fix(low_own, low_got, 0)

    for copy in col_copies:
        copy.wait_recv()

    def spread(x, shift):
        one = jnp.where(lane < group, pltpu.roll(x, LANES - shift, axis=1) if shift else x, 0.0)
        out = one
        for c in range(1, comps):
            out = out + pltpu.roll(one, c * group, axis=1)
        return out

    def column_state(x):
        density, momentum, energy = spread(x, 0), spread(x, 3 * group), spread(x, 4 * group)
        live = lane < comps * group
        density = jnp.where(live, density, 1.0)
        energy = jnp.where(live, energy, 1.0)
        return viscosity(density, energy), momentum / density

    states = {}
    for name, x in (("head", col_own[0]), ("tail", col_own[1]), ("after", col_got[0]), ("before", col_got[1])):
        states[name] = (x, *column_state(x))

    def column_face(a, b):
        (qa, ma, wa), (qb, mb, wb) = states[a], states[b]
        return half_rate * (ma + mb) * (qb - qa) - rate * (wa * qa + wb * qb)

    at_tail = column_face("tail", "after")
    at_head = column_face("before", "head")
    for v, (_, new, c, r) in enumerate(pieces):
        at = (c, tiles - 1, pl.ds(r, SUB), slice(None))
        new[at] = new[at] + jnp.where(lane == LANES - 1, at_tail[:, v:v + 1], 0.0)
        at = (c, 0, pl.ds(r, SUB), slice(None))
        new[at] = new[at] - jnp.where(lane == 0, at_head[:, v:v + 1], 0.0)

    stores = []
    for new, out, low, size in (
        (rotor_new, rotor_out, 0, last_r), (cavity_new, cavity_out, rows, rows_c - rows),
        (rotor_new, rotor_out, last_r, rows), (cavity_new, cavity_out, 0, rows),
    ):
        at = pl.ds(low, size)
        stores.append([
            pltpu.make_async_copy(
                new.at[:, t, at], out.at[:, at, pl.ds(t * LANES, LANES)], store_sem.at[len(stores) * tiles + t])
            for t in range(tiles)
        ])

    def store(index):
        for copy in stores[index]:
            copy.start()

    store(0)
    store(1)

    def seam_fix(region, new, mu, p, ghost):
        for t in range(tiles):
            lanes = pl.ds(t * LANES, LANES)
            factor = half_rate * (viscosity(ghost[t, 0], ghost[t, 4]) + mu[p, :, lanes])
            for c in range(comps):
                at = (c, t, pl.ds(p * rows, rows), slice(None))
                new[at] = new[at] + factor * (ghost[t, c] - region[at])

    wait_blocks(send_c, recv_c, send_c_sem, recv_c_sem, -1, True)
    unpack(recv_c, rotor_ghost, 0)
    seam_fix(rotor, rotor_new, mu_r, planes_r - 1, rotor_ghost)
    store(2)

    landed_shift.wait_recv()
    shifted(two_landed, cavity_ghost, width - offset)
    seam_fix(cavity, cavity_new, mu_c, 0, cavity_ghost)
    store(3)

    cavity_shift.wait_send()
    landed_shift.wait_send()
    wait_blocks(send_r, recv_r, send_r_sem, recv_r_sem, 1, False)
    wait_blocks(send_c, recv_c, send_c_sem, recv_c_sem, -1, False)
    for copy in col_copies:
        copy.wait_send()

    @pl.when(layer < layers - 1)
    def _():
        up_copy.wait_send()

    @pl.when(layer > 0)
    def _():
        down_copy.wait_send()

    for copies in stores:
        for copy in copies:
            copy.wait()


def shards(sectors, rotor_state, cavity_state, block_map, rotor_offset):
    comps, planes_r, rows, width = rotor_state.shape
    planes_c = cavity_state.shape[1]
    tiles = width // LANES
    rotor = rotor_state.reshape(comps, planes_r * rows, width)
    cavity = cavity_state.reshape(comps, planes_c * rows, width)
    f32 = jnp.float32
    edge_rows = comps * tiles * (planes_r + planes_c)
    dma = pltpu.SemaphoreType.DMA
    anywhere = pl.BlockSpec(memory_space=pl.ANY)
    scalar = pl.BlockSpec(memory_space=pltpu.SMEM)
    block = pltpu.VMEM((sectors, 16, LANES), f32)
    tiled_r = pltpu.VMEM((comps, tiles, planes_r * rows, LANES), f32)
    tiled_c = pltpu.VMEM((comps, tiles, planes_c * rows, LANES), f32)
    edge = pltpu.VMEM((edge_rows, LANES), f32)
    columns = pltpu.VMEM((2, SUB, LANES), f32)
    rotor_next, cavity_next = pl.pallas_call(
        kernel,
        out_shape=(jax.ShapeDtypeStruct(rotor.shape, f32), jax.ShapeDtypeStruct(cavity.shape, f32)),
        in_specs=[scalar, scalar, anywhere, anywhere],
        out_specs=(anywhere, anywhere),
        scratch_shapes=[
            tiled_r, tiled_c, tiled_r, tiled_c,
            pltpu.VMEM((planes_r, rows, width), f32), pltpu.VMEM((planes_c, rows, width), f32),
            pltpu.VMEM((planes_r, rows, width), f32), pltpu.VMEM((planes_c, rows, width), f32),
            pltpu.VMEM((2 * tiles, comps, rows, LANES), f32), pltpu.VMEM((2 * tiles, comps, rows, LANES), f32),
            pltpu.VMEM((tiles, comps, rows, LANES), f32), pltpu.VMEM((tiles, comps, rows, LANES), f32),
            block, block, block, block, block,
            edge, edge, edge, edge, columns, columns,
            pltpu.SMEM((sectors,), jnp.int32),
            dma((4 * tiles,)), dma((4 * tiles,)), dma((sectors,)), dma((sectors,)), dma((sectors,)), dma((sectors,)),
            dma((2,)), dma((2,)), dma((4,)), dma((4,)),
        ],
        compiler_params=pltpu.CompilerParams(collective_id=0, has_side_effects=True),
    )(block_map, rotor_offset, rotor, cavity)
    return rotor_next.reshape(rotor_state.shape), cavity_next.reshape(cavity_state.shape)


def solution(mesh):
    placed = (P(None, None, "layer", "sector"), P(None, None, "layer", "sector"), P(), P())
    return jax.shard_map(
        functools.partial(shards, mesh.shape["sector"]),
        mesh=mesh,
        in_specs=placed,
        out_specs=(P(None, None, "layer", "sector"), P(None, None, "layer", "sector")),
        check_vma=False,
    )
```

time: 521 us -> 43.1 us (0.08)
  waiting for transfers between devices: 418 us -> 0 us
  Pallas kernels: 0 us -> 38.2 us
  starting transfers between devices: 36.7 us -> 0 us
  local copies, waits for them, and re-layouts: 29.2 us -> 3.44 us
  other arithmetic: 19.2 us -> 0 us
  between operations: 15.1 us -> 1.29 us
    all_gather x2 -> x0, waiting for transfers between devices: 403 us -> none  [the longest x1 225 us: shards(): every_cavity = lax.all_gather(lifted, 'sector', axis=2, tiled=True)]
    pallas_call x0 -> x1, Pallas kernels: none -> 38.2 us  [shards(): pl.pallas_call(kernel, out_shape=(jax.ShapeDtypeStruct(rotor.shape, f32),...]
    ppermute x10 -> x0, starting transfers between devices: 36.6 us -> none  [the longest x4 20.1 us: with_halo(): lax.ppermute(head, axis, [((i + 1) % count, i) for i in range(ends)])]
    ppermute x10 -> x0, waiting for transfers between devices: 14.9 us -> none  [the longest x4 8.84 us: with_halo(): lax.ppermute(tail, axis, [(i, (i + 1) % count) for i in range(ends)])]
    mul x20 -> x0, other arithmetic: 8.54 us -> none  [the longest x2 3.07 us: region_update(): carried = velocity[None] * cycle_padded]
    gather x2 -> x0, local copies, waits for them, and re-layouts: 6.02 us -> none  [the longest x1 3.02 us: shards(): jnp.take(every_cavity, (position + block_map) % sectors * sectors + slot_...]
  transfers between devices with their start and end apart: 12 -> 0, of which waited for: 5 -> 0; matrix products, arithmetic and copies ran while one was open for 5% -> 0% of each run, Pallas kernels for 0% -> 0%
where the time goes in v1:
time: 43.1 us; the launch traced here: 42.9 us
  Pallas kernels  38.2 us (89%)
  local copies, waits for them, and re-layouts  3.44 us (8%)
  between operations  1.29 us (3%)
    pallas_call x1, Pallas kernels, shards(): pl.pallas_call(kernel, out_shape=(jax.ShapeDtypeStruct(rotor.shape, f32),...  38.2 us
    unnamed x4, local copies, waits for them, and re-layouts  3.44 us

profile of v1, /device:TPU:8, one launch (start us, length us, event | category | flops | bytes accessed | tf_op | source)
XLA Modules:
  0.0 42.9 jit_solution(11112993332097481320)
XLA Ops:
  1.3 38.2 %shard_map.59 = (f32[5,128,512]{2,1,0:T(8,128)}, f32[5,64,512]{2,1,0:T(8,128)}) custom-call(s32[32]{0:T(128)} %map_ref.1, s32[1]{0:T(128)S(6)} %copy.8.offset_ref, f32[5,128,512]{2,1,0:T(8,128)} %bitcast.4, f32[5,64,512]{2,1,0:T(8,128)} %bitcast.6), custom_call_target="tpu_custom_call" | custom-call | tf_op jit(solution)/shard_map/pallas_call | solution.py:430
  39.5 0.0 copy-start
  39.5 2.6 %copy.9 = f32[5,8,16,512]{3,2,1,0:T(8,128)} copy(f32[5,8,16,512]{3,2,1,0:T(8,128)} %bitcast.5) | data formatting | bytes 2621440
  42.1 0.0 copy-done
  42.1 0.8 %copy.10 = f32[5,4,16,512]{3,2,1,0:T(8,128)} copy(f32[5,4,16,512]{3,2,1,0:T(8,128)S(1)} %bitcast.7) | data formatting | bytes 1310720
Async XLA Ops:
  39.5 2.6 %copy-start = (f32[5,64,512]{2,1,0:T(8,128)S(1)}, f32[5,64,512]{2,1,0:T(8,128)}, u32[]{:S(2)}) copy-start(f32[5,64,512]{2,1,0:T(8,128)} %get-tuple-element.5) | copy-start | bytes 1966084

commit v2 on v1

v2 whole, which is shorter than its diff:
```python
import functools

import jax
import jax.numpy as jnp
from jax import lax
from jax.experimental import pallas as pl
from jax.experimental.pallas import tpu as pltpu
from jax.sharding import PartitionSpec as P

DIFFUSION = 0.05
LANES = 128
SUB = 8
PAD = 8
PIECES = 10
EARLY = 2
MESH = pl.DeviceIdType.MESH


def viscosity(density, energy):
    return 0.5 * jnp.exp(0.7 * jnp.log(energy / density))


def iota(axis):
    return lax.broadcasted_iota(jnp.int32, (SUB, LANES), axis)


def granule_transpose(x):
    sub, granule = iota(0), iota(1) // 16
    for bit in range(3):
        s, g = 1 << bit, 16 << bit
        a = (sub // s) % 2
        b = (granule // s) % 2
        up = pltpu.roll(pltpu.roll(x, g, axis=1), SUB - s, axis=0)
        down = pltpu.roll(pltpu.roll(x, LANES - g, axis=1), s, axis=0)
        x = jnp.where(a == b, x, jnp.where(b == 1, up, down))
    return x


def kernel(
    map_hbm, offset_ref, rotor_hbm, cavity_hbm, rotor_new, cavity_new,
    rotor, cavity, mu_r, mu_c, w_r, w_c,
    two_cavity, two_landed, rotor_ghost, cavity_ghost,
    packed, send_r, recv_r, send_c, recv_c,
    low_own, high_own, low_got, high_got, col_own, col_got, inverse_v, inverse,
    map_ref, load_sem, send_r_sem, recv_r_sem, send_c_sem, recv_c_sem, shift_send, shift_recv, edge_send, edge_recv,
    col_send, col_recv,
):
    sectors = lax.axis_size("sector")
    layers = lax.axis_size("layer")
    me = lax.axis_index("sector")
    layer = lax.axis_index("layer")
    comps, tiles, rows_r, _ = rotor_new.shape
    rows_c = cavity_new.shape[2]
    rows = two_cavity.shape[2]
    width = tiles * LANES
    planes_r, planes_c = rows_r // rows, rows_c // rows
    last_r = rows_r - rows
    used = comps * 2
    slot_rows = send_r.shape[1]
    packed_rows = packed.reshape(sectors * slot_rows, LANES)

    def sector_at(step):
        return {"sector": lax.rem(me + step + sectors, sectors)}

    loads = []
    for t in range(tiles):
        loads.append(pltpu.make_async_copy(
            rotor_hbm.at[:, pl.ds(last_r, rows), pl.ds(t * LANES, LANES)], two_landed.at[t], load_sem.at[t]))
    for t in range(tiles):
        loads.append(pltpu.make_async_copy(
            cavity_hbm.at[:, pl.ds(0, rows), pl.ds(t * LANES, LANES)], two_cavity.at[t], load_sem.at[tiles + t]))
    for hbm, region, base in ((rotor_hbm, rotor, 2 * tiles), (cavity_hbm, cavity, 3 * tiles)):
        for t in range(tiles):
            loads.append(pltpu.make_async_copy(
                hbm.at[:, :, pl.ds(t * LANES, LANES)], region.at[:, t, pl.ds(PAD, hbm.shape[1])], load_sem.at[base + t]))
    map_load = pltpu.make_async_copy(map_hbm, map_ref, load_sem.at[4 * tiles + 1])
    map_load.start()
    for copy in loads:
        copy.start()

    barrier = pltpu.get_barrier_semaphore()

    def greet(k, carry):
        pl.semaphore_signal(barrier, inc=1, device_id=sector_at(k), device_id_type=MESH)
        return carry

    lax.fori_loop(1, sectors, greet, 0)

    @pl.when(layer > 0)
    def _():
        pl.semaphore_signal(barrier, inc=1, device_id={"layer": layer - 1}, device_id_type=MESH)

    @pl.when(layer < layers - 1)
    def _():
        pl.semaphore_signal(barrier, inc=1, device_id={"layer": layer + 1}, device_id_type=MESH)

    map_load.wait()

    found = jnp.zeros((SUB, LANES), jnp.int32)
    for j in range(sectors):
        found = jnp.where(iota(1) == map_ref[j], j, found)
    inverse_v[...] = found

    for region in (rotor, cavity):
        for c in range(comps):
            for t in range(tiles):
                region[c, t, pl.ds(0, PAD), :] = jnp.zeros((PAD, LANES), jnp.float32)
                region[c, t, pl.ds(region.shape[2] - PAD, PAD), :] = jnp.zeros((PAD, LANES), jnp.float32)

    to_scalar = pltpu.make_async_copy(inverse_v, inverse, load_sem.at[4 * tiles])
    to_scalar.start()

    def pack(read, send, recv):
        def one(t, carry):
            for q in range(used):
                packed_rows[pl.ds(SUB * slot_rows * t + q, SUB, stride=slot_rows), :] = granule_transpose(read(t, q))
            return carry

        lax.fori_loop(0, tiles, one, 0)

        recv[0] = packed[inverse[0, 0]]

        def slot(k, carry):
            send[k] = packed[inverse[0, k]]
            return carry

        lax.fori_loop(1, sectors, slot, 0)

    def unpack(recv, write):
        def block(j, carry):
            packed[j] = recv[map_ref[j]]
            return carry

        lax.fori_loop(0, sectors, block, 0)

        def one(t, carry):
            for q in range(used):
                write(t, q, granule_transpose(packed_rows[pl.ds(SUB * slot_rows * t + q, SUB, stride=slot_rows), :]))
            return carry

        lax.fori_loop(0, tiles, one, 0)

    def seam_reader(buffer):
        return lambda t, q: buffer[t, q // 2, pl.ds(SUB * (q % 2), SUB), :]

    def seam_writer(buffer, base):
        def write(t, q, value):
            buffer[base + t, q // 2, pl.ds(SUB * (q % 2), SUB), :] = value

        return write

    def block_copy(send, recv, send_sem, recv_sem, k, sign):
        return pltpu.make_async_remote_copy(
            src_ref=send.at[k, pl.ds(0, used)], dst_ref=recv.at[k, pl.ds(0, used)],
            send_sem=send_sem.at[k], recv_sem=recv_sem.at[k],
            device_id=sector_at(sign * k), device_id_type=MESH)

    def start_blocks(send, recv, send_sem, recv_sem, sign):
        def one(k, carry):
            block_copy(send, recv, send_sem, recv_sem, k, sign).start()
            return carry

        lax.fori_loop(1, sectors, one, 0)

    def wait_blocks(send, recv, send_sem, recv_sem, sign, arrived):
        def one(k, carry):
            copy = block_copy(send, recv, send_sem, recv_sem, k, sign)
            if arrived:
                copy.wait_recv()
            else:
                copy.wait_send()
            return carry

        lax.fori_loop(1, sectors, one, 0)

    def shift_copy(buffer, source, target, index, step):
        return pltpu.make_async_remote_copy(
            src_ref=buffer.at[pl.ds(source, tiles)], dst_ref=buffer.at[pl.ds(target, tiles)],
            send_sem=shift_send.at[index], recv_sem=shift_recv.at[index],
            device_id=sector_at(step), device_id_type=MESH)

    def shifted(buffer, target, start):
        tile0 = lax.div(start, jnp.int32(LANES))
        rest = lax.rem(start, jnp.int32(LANES))
        back = lax.rem(LANES - rest, jnp.int32(LANES))
        keep = lax.broadcasted_iota(jnp.int32, (rows, LANES), 1) < LANES - rest
        for t in range(tiles):
            i0 = tile0 + t
            i1 = jnp.minimum(i0 + 1, 2 * tiles - 1)
            for c in range(comps):
                here = pltpu.roll(buffer[i0, c], back, axis=1)
                after = pltpu.roll(buffer[i1, c], back, axis=1)
                target[t, c] = jnp.where(keep, here, after)

    offset = offset_ref[0]

    for t in range(tiles):
        loads[t].wait()
    to_scalar.wait()
    pack(seam_reader(two_landed), send_r, recv_r)
    for t in range(tiles):
        loads[tiles + t].wait()

    for copy in loads[2 * tiles:]:
        copy.wait()

    first_c = comps * tiles * planes_r
    for edge, own in ((0, low_own), (rows - 1, high_own)):
        for c in range(comps):
            for t in range(tiles):
                own[pl.ds((c * tiles + t) * planes_r, planes_r), :] = rotor[c, t, pl.ds(PAD + edge, planes_r, stride=rows), :]
                own[pl.ds(first_c + (c * tiles + t) * planes_c, planes_c), :] = cavity[
                    c, t, pl.ds(PAD + edge, planes_c, stride=rows), :]

    lane = iota(1)
    pieces = []
    for c in range(comps):
        for region, new, planes in ((rotor, rotor_new, planes_r), (cavity, cavity_new, planes_c)):
            for p in range(planes):
                for half in range(2):
                    pieces.append((region, new, c, p * rows + half * SUB))
    group = len(pieces) // comps
    zero = jnp.zeros((SUB, LANES), jnp.float32)
    head, tail = zero, zero
    for v, (region, _, c, r) in enumerate(pieces):
        head = jnp.where(lane == v, region[c, 0, pl.ds(PAD + r, SUB), :][:, 0:1], head)
        tail = jnp.where(lane == v, region[c, tiles - 1, pl.ds(PAD + r, SUB), :][:, LANES - 1:], tail)
    col_own[0] = head
    col_own[1] = tail
    pl.semaphore_wait(barrier, sectors - 1 + jnp.where(layer > 0, 1, 0) + jnp.where(layer < layers - 1, 1, 0))

    cavity_shift = shift_copy(two_cavity, 0, tiles, 0, -1)
    cavity_shift.start()
    start_blocks(send_r, recv_r, send_r_sem, recv_r_sem, 1)

    col_copies = [
        pltpu.make_async_remote_copy(
            src_ref=col_own.at[i], dst_ref=col_got.at[i], send_sem=col_send.at[i], recv_sem=col_recv.at[i],
            device_id=sector_at(-1 if i == 0 else 1), device_id_type=MESH)
        for i in range(2)
    ]
    for copy in col_copies:
        copy.start()

    edge_rows = low_own.shape[0] // PIECES

    def edge_copy(upward, piece, step):
        source, target = (high_own, low_got) if upward else (low_own, high_got)
        at = pl.ds(piece * edge_rows, edge_rows)
        return pltpu.make_async_remote_copy(
            src_ref=source.at[at], dst_ref=target.at[at],
            send_sem=edge_send.at[upward, piece], recv_sem=edge_recv.at[upward, piece],
            device_id={"layer": lax.rem(layer + step + layers, layers)}, device_id_type=MESH)

    def start_edges(low, high):
        @pl.when(layer < layers - 1)
        def _():
            for piece in range(low, high):
                edge_copy(1, piece, 1).start()

        @pl.when(layer > 0)
        def _():
            for piece in range(low, high):
                edge_copy(0, piece, -1).start()

    start_edges(0, EARLY)

    rate = jnp.float32(DIFFUSION)
    half_rate = jnp.float32(0.5 * DIFFUSION)
    row = lax.broadcasted_iota(jnp.int32, (rows, LANES), 0)
    column = lax.broadcasted_iota(jnp.int32, (rows, LANES), 1)

    def interior(region, new, mu, w, planes):
        def first(p, carry):
            at = pl.ds(pl.multiple_of(PAD + p * rows, SUB), rows)
            for t in range(tiles):
                density = region[0, t, at, :]
                mu[t, at, :] = viscosity(density, region[4, t, at, :])
                w[t, at, :] = region[3, t, at, :] / density
            return carry

        lax.fori_loop(0, planes, first, 0)

        def one(p, carry):
            base = pl.multiple_of(PAD + p * rows, SUB)
            at = pl.ds(base, rows)
            upper, lower = pl.ds(base + 1, rows), pl.ds(base - 1, rows)
            above = pl.ds(pl.multiple_of(PAD + jnp.minimum(p + 1, planes - 1) * rows, SUB), rows)
            below = pl.ds(pl.multiple_of(PAD + jnp.maximum(p - 1, 0) * rows, SUB), rows)
            rate_above = jnp.where(p < planes - 1, half_rate, 0.0)
            rate_below = jnp.where(p > 0, half_rate, 0.0)

            def after(ref, t):
                x = ref[t, at, :]
                if t < tiles - 1:
                    x = jnp.where(column == 0, ref[t + 1, at, :], x)
                return pltpu.roll(x, LANES - 1, axis=1)

            def before(ref, t):
                x = ref[t, at, :]
                if t > 0:
                    x = jnp.where(column == LANES - 1, ref[t - 1, at, :], x)
                return pltpu.roll(x, 1, axis=1)

            for t in range(tiles):
                m = mu[t, at, :]
                up = rate_above * (m + mu[t, above, :])
                down = rate_below * (m + mu[t, below, :])
                out = jnp.where(row == rows - 1, 0.0, half_rate * (m + mu[t, upper, :]))
                inn = jnp.where(row == 0, 0.0, half_rate * (m + mu[t, lower, :]))
                east = half_rate * (m + after(mu, t))
                west = half_rate * (m + before(mu, t))
                wind_east = rate * after(w, t)
                wind_west = rate * before(w, t)
                if t == tiles - 1:
                    east = jnp.where(column == LANES - 1, 0.0, east)
                    wind_east = jnp.where(column == LANES - 1, 0.0, wind_east)
                if t == 0:
                    west = jnp.where(column == 0, 0.0, west)
                    wind_west = jnp.where(column == 0, 0.0, wind_west)
                centre = 1.0 - ((up + down) + (out + inn) + (east + west))
                east = east - wind_east
                west = west + wind_west
                for c in range(comps):
                    values = region.at[c]
                    total = centre * values[t, at, :]
                    total = total + (up * values[t, above, :] + down * values[t, below, :])
                    total = total + (out * values[t, upper, :] + inn * values[t, lower, :])
                    total = total + (east * after(values, t) + west * before(values, t))
                    new[c, t, pl.ds(pl.multiple_of(p * rows, rows), rows), :] = total
            return carry

        lax.fori_loop(0, planes, one, 0)

    interior(rotor, rotor_new, mu_r, w_r, planes_r)
    interior(cavity, cavity_new, mu_c, w_c, planes_c)

    cavity_shift.wait_recv()
    shifted(two_cavity, rotor_ghost, offset)
    pack(seam_reader(rotor_ghost), send_c, recv_c)
    start_blocks(send_c, recv_c, send_c_sem, recv_c_sem, -1)

    wait_blocks(send_r, recv_r, send_r_sem, recv_r_sem, 1, True)
    unpack(recv_r, seam_writer(two_landed, tiles))
    landed_shift = shift_copy(two_landed, tiles, 0, 1, 1)
    landed_shift.start()
    start_edges(EARLY, PIECES)

    def edge_fix(own, got, edge):
        for region, new, planes, base in ((rotor, rotor_new, planes_r, 0), (cavity, cavity_new, planes_c, first_c)):
            size = tiles * planes
            a = [own[pl.ds(base + c * size, size), :] for c in range(comps)]
            b = [got[pl.ds(base + c * size, size), :] for c in range(comps)]
            factor = half_rate * (viscosity(a[0], a[4]) + viscosity(b[0], b[4]))
            for c in range(comps):
                change = factor * (b[c] - a[c])
                for t in range(tiles):
                    at = (c, t, pl.ds(edge, planes, stride=rows), slice(None))
                    new[at] = new[at] + change[t * planes:(t + 1) * planes]

    for copy in col_copies:
        copy.wait_recv()

    def spread(x, shift):
        one = jnp.where(lane < group, pltpu.roll(x, LANES - shift, axis=1) if shift else x, 0.0)
        out = one
        for c in range(1, comps):
            out = out + pltpu.roll(one, c * group, axis=1)
        return out

    def column_state(x):
        density, momentum, energy = spread(x, 0), spread(x, 3 * group), spread(x, 4 * group)
        live = lane < comps * group
        density = jnp.where(live, density, 1.0)
        energy = jnp.where(live, energy, 1.0)
        return viscosity(density, energy), momentum / density

    states = {}
    for name, x in (("head", col_own[0]), ("tail", col_own[1]), ("after", col_got[0]), ("before", col_got[1])):
        states[name] = (x, *column_state(x))

    def column_face(a, b):
        (qa, ma, wa), (qb, mb, wb) = states[a], states[b]
        return half_rate * (ma + mb) * (qb - qa), rate * wb * qb

    def column_change(own, other, sign):
        diffused, carried = column_face(own, other)
        return diffused - sign * carried

    at_tail = column_change("tail", "after", 1.0)
    at_head = column_change("head", "before", -1.0)
    for v, (_, new, c, r) in enumerate(pieces):
        at = (c, tiles - 1, pl.ds(r, SUB), slice(None))
        new[at] = new[at] + jnp.where(lane == LANES - 1, at_tail[:, v:v + 1], 0.0)
        at = (c, 0, pl.ds(r, SUB), slice(None))
        new[at] = new[at] + jnp.where(lane == 0, at_head[:, v:v + 1], 0.0)

    def seam_fix(region, new, mu, p, ghost):
        for t in range(tiles):
            inside = pl.ds(PAD + p * rows, rows)
            factor = half_rate * (viscosity(ghost[t, 0], ghost[t, 4]) + mu[t, inside, :])
            for c in range(comps):
                at = (c, t, pl.ds(p * rows, rows), slice(None))
                new[at] = new[at] + factor * (ghost[t, c] - region[c, t, inside, :])

    wait_blocks(send_c, recv_c, send_c_sem, recv_c_sem, -1, True)
    unpack(recv_c, seam_writer(rotor_ghost, 0))
    seam_fix(rotor, rotor_new, mu_r, planes_r - 1, rotor_ghost)

    landed_shift.wait_recv()
    shifted(two_landed, cavity_ghost, width - offset)
    seam_fix(cavity, cavity_new, mu_c, 0, cavity_ghost)

    @pl.when(layer < layers - 1)
    def _():
        for piece in range(PIECES):
            edge_copy(0, piece, 1).wait_recv()
        edge_fix(high_own, high_got, rows - 1)

    @pl.when(layer > 0)
    def _():
        for piece in range(PIECES):
            edge_copy(1, piece, -1).wait_recv()
        edge_fix(low_own, low_got, 0)

    cavity_shift.wait_send()
    landed_shift.wait_send()
    wait_blocks(send_r, recv_r, send_r_sem, recv_r_sem, 1, False)
    wait_blocks(send_c, recv_c, send_c_sem, recv_c_sem, -1, False)
    for copy in col_copies:
        copy.wait_send()

    @pl.when(layer < layers - 1)
    def _():
        for piece in range(PIECES):
            edge_copy(1, piece, 1).wait_send()

    @pl.when(layer > 0)
    def _():
        for piece in range(PIECES):
            edge_copy(0, piece, -1).wait_send()


def relay(rotor_in, cavity_in, rotor_out, cavity_out, sem):
    copies = []
    for source, target in ((rotor_in, rotor_out), (cavity_in, cavity_out)):
        for t in range(source.shape[1]):
            copies.append(pltpu.make_async_copy(
                source.at[:, t], target.at[:, :, pl.ds(t * LANES, LANES)], sem.at[len(copies)]))
    for copy in copies:
        copy.start()
    for copy in copies:
        copy.wait()


def shards(sectors, rotor_state, cavity_state, block_map, rotor_offset):
    comps, planes_r, rows, width = rotor_state.shape
    planes_c = cavity_state.shape[1]
    tiles = width // LANES
    rotor = rotor_state.reshape(comps, planes_r * rows, width)
    cavity = cavity_state.reshape(comps, planes_c * rows, width)
    f32 = jnp.float32
    edge_rows = comps * tiles * (planes_r + planes_c)
    dma = pltpu.SemaphoreType.DMA
    hbm = pl.BlockSpec(memory_space=pltpu.HBM)
    anywhere = pl.BlockSpec(memory_space=pl.ANY)
    block = pltpu.VMEM((sectors, 16, LANES), f32)
    resident = pl.BlockSpec(memory_space=pltpu.VMEM)
    shape_r, shape_c = (comps, tiles, planes_r * rows, LANES), (comps, tiles, planes_c * rows, LANES)
    held_r, held_c = planes_r * rows + 2 * PAD, planes_c * rows + 2 * PAD
    edge = pltpu.VMEM((edge_rows, LANES), f32)
    columns = pltpu.VMEM((2, SUB, LANES), f32)
    rotor_new, cavity_new = pl.pallas_call(
        kernel,
        out_shape=(jax.ShapeDtypeStruct(shape_r, f32), jax.ShapeDtypeStruct(shape_c, f32)),
        in_specs=[hbm, pl.BlockSpec(memory_space=pltpu.SMEM), hbm, hbm],
        out_specs=(resident, resident),
        scratch_shapes=[
            pltpu.VMEM((comps, tiles, held_r, LANES), f32), pltpu.VMEM((comps, tiles, held_c, LANES), f32),
            pltpu.VMEM((tiles, held_r, LANES), f32), pltpu.VMEM((tiles, held_c, LANES), f32),
            pltpu.VMEM((tiles, held_r, LANES), f32), pltpu.VMEM((tiles, held_c, LANES), f32),
            pltpu.VMEM((2 * tiles, comps, rows, LANES), f32), pltpu.VMEM((2 * tiles, comps, rows, LANES), f32),
            pltpu.VMEM((tiles, comps, rows, LANES), f32), pltpu.VMEM((tiles, comps, rows, LANES), f32),
            block, block, block, block, block,
            edge, edge, edge, edge, columns, columns,
            pltpu.VMEM((SUB, LANES), jnp.int32), pltpu.SMEM((SUB, LANES), jnp.int32),
            pltpu.SMEM((sectors,), jnp.int32),
            dma((4 * tiles + 2,)), dma((sectors,)), dma((sectors,)), dma((sectors,)), dma((sectors,)),
            dma((2,)), dma((2,)), dma((2, PIECES)), dma((2, PIECES)), dma((2,)), dma((2,)),
        ],
        compiler_params=pltpu.CompilerParams(
            collective_id=0, has_side_effects=True, vmem_limit_bytes=24 * 1024 * 1024),
    )(pltpu.with_memory_space_constraint(block_map, pltpu.HBM), rotor_offset,
      *(pltpu.with_memory_space_constraint(x, pltpu.HBM) for x in (rotor, cavity)))
    rotor_next, cavity_next = pl.pallas_call(
        relay,
        out_shape=(jax.ShapeDtypeStruct(rotor.shape, f32), jax.ShapeDtypeStruct(cavity.shape, f32)),
        in_specs=[anywhere, anywhere],
        out_specs=(hbm, hbm),
        scratch_shapes=[dma((2 * tiles,))],
        compiler_params=pltpu.CompilerParams(vmem_limit_bytes=1024 * 1024),
    )(rotor_new, cavity_new)
    return rotor_next.reshape(rotor_state.shape), cavity_next.reshape(cavity_state.shape)


def solution(mesh):
    placed = (P(None, None, "layer", "sector"), P(None, None, "layer", "sector"), P(), P())
    return jax.shard_map(
        functools.partial(shards, mesh.shape["sector"]),
        mesh=mesh,
        in_specs=placed,
        out_specs=(P(None, None, "layer", "sector"), P(None, None, "layer", "sector")),
        check_vma=False,
    )
```

time: 43.1 us -> 37.7 us (0.87)
  local copies, waits for them, and re-layouts: 3.44 us -> 0 us
  Pallas kernels: 38.2 us -> 36.3 us
    unnamed x4 -> x0, local copies, waits for them, and re-layouts: 3.44 us -> none
    pallas_call x1 -> x2, Pallas kernels: 38.2 us -> 36.3 us  [the longest x1 34.9 us: shards(): pl.pallas_call(kernel, out_shape=(jax.ShapeDtypeStruct(shape_r, f32), jax...]
where the time goes in v2:
time: 37.7 us; the launch traced here: 37.6 us
  Pallas kernels  36.3 us (96%)
  between operations  1.29 us (3%)
    pallas_call x1, Pallas kernels, shards(): pl.pallas_call(kernel, out_shape=(jax.ShapeDtypeStruct(shape_r, f32), jax...  34.9 us
    pallas_call x1, Pallas kernels, shards(): pl.pallas_call(relay, out_shape=(jax.ShapeDtypeStruct(rotor.shape, f32),...  1.33 us

profile of v2, /device:TPU:8, one launch (start us, length us, event | category | flops | bytes accessed | tf_op | source)
XLA Modules:
  0.0 37.6 jit_solution(10046324015619061910)
XLA Ops:
  1.3 34.9 %shard_map.59 = (f32[5,4,128,128]{3,2,1,0:T(8,128)S(1)}, f32[5,4,64,128]{3,2,1,0:T(8,128)S(1)}) custom-call(s32[32]{0:T(128)} %map_hbm.1, s32[1]{0:T(128)S(6)} %copy.6.offset_ref, f32[5,128,512]{2,1,0:T(8,128)} %bitcast.4, f32[5,64,512]{2,1,0:T(8,128)} %bitcast.5), custom_call_target="tpu_custom_call" | custom-call | tf_op jit(solution)/shard_map/pallas_call | solution.py:473
  36.2 1.3 %shard_map.60 = (f32[5,128,512]{2,1,0:T(8,128)}, f32[5,64,512]{2,1,0:T(8,128)}) custom-call(f32[5,4,128,128]{3,2,1,0:T(8,128)S(1)} %get-tuple-element.6.rotor_in, f32[5,4,64,128]{3,2,1,0:T(8,128)S(1)} %get-tuple-element.7.cavity_in), custom_call_target="tpu_custom_call" | custom-call | tf_op jit(solution)/shard_map/pallas_call | solution.py:495

commit v3 on v2

--- a/solution.py
+++ b/solution.py
@@ -11,8 +11,9 @@
 LANES = 128
 SUB = 8
 PAD = 8
-PIECES = 10
-EARLY = 2
+EDGE_ORDER = (0, 4, 1, 2, 3)
+FIRST = 1
+SECOND = 1
 MESH = pl.DeviceIdType.MESH
 
 
@@ -62,6 +63,23 @@
     def sector_at(step):
         return {"sector": lax.rem(me + step + sectors, sectors)}
 
+    barrier = pltpu.get_barrier_semaphore()
+
+    @pl.when(layer > 0)
+    def _():
+        pl.semaphore_signal(barrier, inc=1, device_id={"layer": layer - 1}, device_id_type=MESH)
+
+    @pl.when(layer < layers - 1)
+    def _():
+        pl.semaphore_signal(barrier, inc=1, device_id={"layer": layer + 1}, device_id_type=MESH)
+
+
+    def greet(k, carry):
+        pl.semaphore_signal(barrier, inc=1, device_id=sector_at(k), device_id_type=MESH)
+        return carry
+
+    lax.fori_loop(1, sectors, greet, 0)
+
     loads = []
     for t in range(tiles):
         loads.append(pltpu.make_async_copy(
@@ -78,38 +96,6 @@
     for copy in loads:
         copy.start()
 
-    barrier = pltpu.get_barrier_semaphore()
-
-    def greet(k, carry):
-        pl.semaphore_signal(barrier, inc=1, device_id=sector_at(k), device_id_type=MESH)
-        return carry
-
-    lax.fori_loop(1, sectors, greet, 0)
-
-    @pl.when(layer > 0)
-    def _():
-        pl.semaphore_signal(barrier, inc=1, device_id={"layer": layer - 1}, device_id_type=MESH)
-
-    @pl.when(layer < layers - 1)
-    def _():
-        pl.semaphore_signal(barrier, inc=1, device_id={"layer": layer + 1}, device_id_type=MESH)
-
-    map_load.wait()
-
-    found = jnp.zeros((SUB, LANES), jnp.int32)
-    for j in range(sectors):
-        found = jnp.where(iota(1) == map_ref[j], j, found)
-    inverse_v[...] = found
-
-    for region in (rotor, cavity):
-        for c in range(comps):
-            for t in range(tiles):
-                region[c, t, pl.ds(0, PAD), :] = jnp.zeros((PAD, LANES), jnp.float32)
-                region[c, t, pl.ds(region.shape[2] - PAD, PAD), :] = jnp.zeros((PAD, LANES), jnp.float32)
-
-    to_scalar = pltpu.make_async_copy(inverse_v, inverse, load_sem.at[4 * tiles])
-    to_scalar.start()
-
     def pack(read, send, recv):
         def one(t, carry):
             for q in range(used):
@@ -194,23 +180,65 @@
 
     offset = offset_ref[0]
 
+    def edge_copy(upward, c, step):
+        source, target = (high_own, low_got) if upward else (low_own, high_got)
+        at = pl.ds(c * piece, piece)
+        return pltpu.make_async_remote_copy(
+            src_ref=source.at[at], dst_ref=target.at[at],
+            send_sem=edge_send.at[upward, c], recv_sem=edge_recv.at[upward, c],
+            device_id={"layer": lax.rem(layer + step + layers, layers)}, device_id_type=MESH)
+
+    def start_edges(low, high):
+        @pl.when(layer < layers - 1)
+        def _():
+            for c in EDGE_ORDER[low:high]:
+                edge_copy(1, c, 1).start()
+
+        @pl.when(layer > 0)
+        def _():
+            for c in EDGE_ORDER[low:high]:
+                edge_copy(0, c, -1).start()
+
+    map_load.wait()
+
+    found = jnp.zeros((SUB, LANES), jnp.int32)
+    for j in range(sectors):
+        found = jnp.where(iota(1) == map_ref[j], j, found)
+    inverse_v[...] = found
+
+    to_scalar = pltpu.make_async_copy(inverse_v, inverse, load_sem.at[4 * tiles])
+    to_scalar.start()
+
     for t in range(tiles):
         loads[t].wait()
     to_scalar.wait()
     pack(seam_reader(two_landed), send_r, recv_r)
     for t in range(tiles):
         loads[tiles + t].wait()
+    for region in (rotor, cavity):
+        for c in range(comps):
+            for t in range(tiles):
+                region[c, t, pl.ds(0, PAD), :] = jnp.zeros((PAD, LANES), jnp.float32)
+                region[c, t, pl.ds(region.shape[2] - PAD, PAD), :] = jnp.zeros((PAD, LANES), jnp.float32)
+
+    pl.semaphore_wait(barrier, sectors - 1 + jnp.where(layer > 0, 1, 0) + jnp.where(layer < layers - 1, 1, 0))
+
+    cavity_shift = shift_copy(two_cavity, 0, tiles, 0, -1)
+    cavity_shift.start()
+    start_blocks(send_r, recv_r, send_r_sem, recv_r_sem, 1)
 
     for copy in loads[2 * tiles:]:
         copy.wait()
-
-    first_c = comps * tiles * planes_r
+    piece = tiles * (planes_r + planes_c)
+    parts = ((rotor, rotor_new, planes_r, 0), (cavity, cavity_new, planes_c, tiles * planes_r))
     for edge, own in ((0, low_own), (rows - 1, high_own)):
         for c in range(comps):
-            for t in range(tiles):
-                own[pl.ds((c * tiles + t) * planes_r, planes_r), :] = rotor[c, t, pl.ds(PAD + edge, planes_r, stride=rows), :]
-                own[pl.ds(first_c + (c * tiles + t) * planes_c, planes_c), :] = cavity[
-                    c, t, pl.ds(PAD + edge, planes_c, stride=rows), :]
+            for region, _, planes, base in parts:
+                for t in range(tiles):
+                    own[pl.ds(c * piece + base + t * planes, planes), :] = region[
+                        c, t, pl.ds(PAD + edge, planes, stride=rows), :]
+
+    start_edges(0, FIRST)
 
     lane = iota(1)
     pieces = []
@@ -227,12 +255,6 @@
         tail = jnp.where(lane == v, region[c, tiles - 1, pl.ds(PAD + r, SUB), :][:, LANES - 1:], tail)
     col_own[0] = head
     col_own[1] = tail
-    pl.semaphore_wait(barrier, sectors - 1 + jnp.where(layer > 0, 1, 0) + jnp.where(layer < layers - 1, 1, 0))
-
-    cavity_shift = shift_copy(two_cavity, 0, tiles, 0, -1)
-    cavity_shift.start()
-    start_blocks(send_r, recv_r, send_r_sem, recv_r_sem, 1)
-
     col_copies = [
         pltpu.make_async_remote_copy(
             src_ref=col_own.at[i], dst_ref=col_got.at[i], send_sem=col_send.at[i], recv_sem=col_recv.at[i],
@@ -241,29 +263,6 @@
     ]
     for copy in col_copies:
         copy.start()
-
-    edge_rows = low_own.shape[0] // PIECES
-
-    def edge_copy(upward, piece, step):
-        source, target = (high_own, low_got) if upward else (low_own, high_got)
-        at = pl.ds(piece * edge_rows, edge_rows)
-        return pltpu.make_async_remote_copy(
-            src_ref=source.at[at], dst_ref=target.at[at],
-            send_sem=edge_send.at[upward, piece], recv_sem=edge_recv.at[upward, piece],
-            device_id={"layer": lax.rem(layer + step + layers, layers)}, device_id_type=MESH)
-
-    def start_edges(low, high):
-        @pl.when(layer < layers - 1)
-        def _():
-            for piece in range(low, high):
-                edge_copy(1, piece, 1).start()
-
-        @pl.when(layer > 0)
-        def _():
-            for piece in range(low, high):
-                edge_copy(0, piece, -1).start()
-
-    start_edges(0, EARLY)
 
     rate = jnp.float32(DIFFUSION)
     half_rate = jnp.float32(0.5 * DIFFUSION)
@@ -340,23 +339,34 @@
     pack(seam_reader(rotor_ghost), send_c, recv_c)
     start_blocks(send_c, recv_c, send_c_sem, recv_c_sem, -1)
 
+    start_edges(FIRST, SECOND)
+
     wait_blocks(send_r, recv_r, send_r_sem, recv_r_sem, 1, True)
     unpack(recv_r, seam_writer(two_landed, tiles))
     landed_shift = shift_copy(two_landed, tiles, 0, 1, 1)
     landed_shift.start()
-    start_edges(EARLY, PIECES)
-
-    def edge_fix(own, got, edge):
-        for region, new, planes, base in ((rotor, rotor_new, planes_r, 0), (cavity, cavity_new, planes_c, first_c)):
-            size = tiles * planes
-            a = [own[pl.ds(base + c * size, size), :] for c in range(comps)]
-            b = [got[pl.ds(base + c * size, size), :] for c in range(comps)]
-            factor = half_rate * (viscosity(a[0], a[4]) + viscosity(b[0], b[4]))
-            for c in range(comps):
-                change = factor * (b[c] - a[c])
-                for t in range(tiles):
-                    at = (c, t, pl.ds(edge, planes, stride=rows), slice(None))
-                    new[at] = new[at] + change[t * planes:(t + 1) * planes]
+    start_edges(SECOND, comps)
+
+    def edge_factor(own, got, base, size):
+        a, b = ([ref[pl.ds(c * piece + base, size), :] for c in (0, 4)] for ref in (own, got))
+        return half_rate * (viscosity(*a) + viscosity(*b))
+
+    def edge_fix(own, got, edge, c, factors):
+        for (_, new, planes, base), factor in zip(parts, factors):
+            at = pl.ds(c * piece + base, tiles * planes)
+            change = factor * (got[at, :] - own[at, :])
+            for t in range(tiles):
+                at = (c, t, pl.ds(edge, planes, stride=rows), slice(None))
+                new[at] = new[at] + change[t * planes:(t + 1) * planes]
+
+    def edges(own, got, edge, upward, step):
+        for c in EDGE_ORDER[:2]:
+            edge_copy(upward, c, step).wait_recv()
+        factors = [edge_factor(own, got, base, tiles * planes) for _, _, planes, base in parts]
+        for n, c in enumerate(EDGE_ORDER):
+            if n > 1:
+                edge_copy(upward, c, step).wait_recv()
+            edge_fix(own, got, edge, c, factors)
 
     for copy in col_copies:
         copy.wait_recv()
@@ -407,38 +417,34 @@
     unpack(recv_c, seam_writer(rotor_ghost, 0))
     seam_fix(rotor, rotor_new, mu_r, planes_r - 1, rotor_ghost)
 
-    landed_shift.wait_recv()
-    shifted(two_landed, cavity_ghost, width - offset)
-    seam_fix(cavity, cavity_new, mu_c, 0, cavity_ghost)
-
-    @pl.when(layer < layers - 1)
-    def _():
-        for piece in range(PIECES):
-            edge_copy(0, piece, 1).wait_recv()
-        edge_fix(high_own, high_got, rows - 1)
-
-    @pl.when(layer > 0)
-    def _():
-        for piece in range(PIECES):
-            edge_copy(1, piece, -1).wait_recv()
-        edge_fix(low_own, low_got, 0)
-
     cavity_shift.wait_send()
-    landed_shift.wait_send()
     wait_blocks(send_r, recv_r, send_r_sem, recv_r_sem, 1, False)
     wait_blocks(send_c, recv_c, send_c_sem, recv_c_sem, -1, False)
     for copy in col_copies:
         copy.wait_send()
 
+    landed_shift.wait_recv()
+    shifted(two_landed, cavity_ghost, width - offset)
+    seam_fix(cavity, cavity_new, mu_c, 0, cavity_ghost)
+    landed_shift.wait_send()
+
     @pl.when(layer < layers - 1)
     def _():
-        for piece in range(PIECES):
-            edge_copy(1, piece, 1).wait_send()
+        for c in range(comps):
+            edge_copy(1, c, 1).wait_send()
 
     @pl.when(layer > 0)
     def _():
-        for piece in range(PIECES):
-            edge_copy(0, piece, -1).wait_send()
+        for c in range(comps):
+            edge_copy(0, c, -1).wait_send()
+
+    @pl.when(layer < layers - 1)
+    def _():
+        edges(high_own, high_got, rows - 1, 0, 1)
+
+    @pl.when(layer > 0)
+    def _():
+        edges(low_own, low_got, 0, 1, -1)
 
 
 def relay(rotor_in, cavity_in, rotor_out, cavity_out, sem):
@@ -486,7 +492,7 @@
             pltpu.VMEM((SUB, LANES), jnp.int32), pltpu.SMEM((SUB, LANES), jnp.int32),
             pltpu.SMEM((sectors,), jnp.int32),
             dma((4 * tiles + 2,)), dma((sectors,)), dma((sectors,)), dma((sectors,)), dma((sectors,)),
-            dma((2,)), dma((2,)), dma((2, PIECES)), dma((2, PIECES)), dma((2,)), dma((2,)),
+            dma((2,)), dma((2,)), dma((2, comps)), dma((2, comps)), dma((2,)), dma((2,)),
         ],
         compiler_params=pltpu.CompilerParams(
             collective_id=0, has_side_effects=True, vmem_limit_bytes=24 * 1024 * 1024),

time: 37.7 us -> 36.5 us (0.968)
  the two profiles are of different devices: /device:TPU:8 before, /device:TPU:33 now
where the time goes in v3:
time: 36.5 us; the launch traced here: 36.4 us
  Pallas kernels  35.1 us (96%)
  between operations  1.29 us (4%)
    pallas_call x1, Pallas kernels, shards(): pl.pallas_call(kernel, out_shape=(jax.ShapeDtypeStruct(shape_r, f32), jax...  33.7 us
    pallas_call x1, Pallas kernels, shards(): pl.pallas_call(relay, out_shape=(jax.ShapeDtypeStruct(rotor.shape, f32),...  1.33 us

profile of v3, /device:TPU:33, one launch (start us, length us, event | category | flops | bytes accessed | tf_op | source)
XLA Modules:
  0.0 36.4 jit_solution(438745528494868173)
XLA Ops:
  1.3 33.7 %shard_map.59 = (f32[5,4,128,128]{3,2,1,0:T(8,128)S(1)}, f32[5,4,64,128]{3,2,1,0:T(8,128)S(1)}) custom-call(s32[32]{0:T(128)} %map_hbm.1, s32[1]{0:T(128)S(6)} %copy.6.offset_ref, f32[5,128,512]{2,1,0:T(8,128)} %bitcast.4, f32[5,64,512]{2,1,0:T(8,128)} %bitcast.5), custom_call_target="tpu_custom_call" | custom-call | tf_op jit(solution)/shard_map/pallas_call | solution.py:479
  35.0 1.3 %shard_map.60 = (f32[5,128,512]{2,1,0:T(8,128)}, f32[5,64,512]{2,1,0:T(8,128)}) custom-call(f32[5,4,128,128]{3,2,1,0:T(8,128)S(1)} %get-tuple-element.6.rotor_in, f32[5,4,64,128]{3,2,1,0:T(8,128)S(1)} %get-tuple-element.7.cavity_in), custom_call_target="tpu_custom_call" | custom-call | tf_op jit(solution)/shard_map/pallas_call | solution.py:501

commit v4 on v3

--- a/solution.py
+++ b/solution.py
@@ -14,6 +14,7 @@
 EDGE_ORDER = (0, 4, 1, 2, 3)
 FIRST = 1
 SECOND = 1
+RELAYED = (3,)
 MESH = pl.DeviceIdType.MESH
 
 
@@ -44,7 +45,7 @@
     packed, send_r, recv_r, send_c, recv_c,
     low_own, high_own, low_got, high_got, col_own, col_got, inverse_v, inverse,
     map_ref, load_sem, send_r_sem, recv_r_sem, send_c_sem, recv_c_sem, shift_send, shift_recv, edge_send, edge_recv,
-    col_send, col_recv,
+    col_send, col_recv, way_got, way_send, way_recv,
 ):
     sectors = lax.axis_size("sector")
     layers = lax.axis_size("layer")
@@ -73,6 +74,14 @@
     def _():
         pl.semaphore_signal(barrier, inc=1, device_id={"layer": layer + 1}, device_id_type=MESH)
 
+
+    @pl.when(layer == 0)
+    def _():
+        pl.semaphore_signal(barrier, inc=1, device_id={"layer": layer + 2}, device_id_type=MESH)
+
+    @pl.when(layer == layers - 1)
+    def _():
+        pl.semaphore_signal(barrier, inc=1, device_id={"layer": layer - 2}, device_id_type=MESH)
 
     def greet(k, carry):
         pl.semaphore_signal(barrier, inc=1, device_id=sector_at(k), device_id_type=MESH)
@@ -188,16 +197,55 @@
             send_sem=edge_send.at[upward, c], recv_sem=edge_recv.at[upward, c],
             device_id={"layer": lax.rem(layer + step + layers, layers)}, device_id_type=MESH)
 
+    by_way_up, by_way_down = layer == layers - 3, layer == 2
+    way_up, way_down = layer == layers - 1, layer == 0
+    has_up = layer < layers - 1
+    has_down = layer > 0
+
+    def way_copy(upward, n):
+        source = high_own if upward else low_own
+        return pltpu.make_async_remote_copy(
+            src_ref=source.at[pl.ds(RELAYED[n] * piece, piece)], dst_ref=way_got.at[pl.ds(n * piece, piece)],
+            send_sem=way_send.at[n], recv_sem=way_recv.at[n],
+            device_id={"layer": lax.rem(layer + (2 if upward else -2) + layers, layers)}, device_id_type=MESH)
+
+    def way_pass(upward, n):
+        target = low_got if upward else high_got
+        return pltpu.make_async_remote_copy(
+            src_ref=way_got.at[pl.ds(n * piece, piece)], dst_ref=target.at[pl.ds(RELAYED[n] * piece, piece)],
+            send_sem=way_send.at[n], recv_sem=edge_recv.at[upward, RELAYED[n]],
+            device_id={"layer": lax.rem(layer + (-1 if upward else 1) + layers, layers)}, device_id_type=MESH)
+
+    def each_way(upward, at, act):
+        @pl.when(at)
+        def _():
+            for n in range(len(RELAYED)):
+                act(upward, n)
+
+    def each_edge(group, act):
+        direct = [c for c in group if c not in RELAYED]
+        others = [c for c in group if c in RELAYED]
+        for upward, has, by_way, step in ((1, has_up, by_way_up, 1), (0, has_down, by_way_down, -1)):
+            @pl.when(has)
+            def _():
+                for c in direct:
+                    act(edge_copy(upward, c, step))
+
+            if others:
+                @pl.when(jnp.logical_and(has, jnp.logical_not(by_way)))
+                def _():
+                    for c in others:
+                        act(edge_copy(upward, c, step))
+
     def start_edges(low, high):
-        @pl.when(layer < layers - 1)
-        def _():
-            for c in EDGE_ORDER[low:high]:
-                edge_copy(1, c, 1).start()
-
-        @pl.when(layer > 0)
-        def _():
-            for c in EDGE_ORDER[low:high]:
-                edge_copy(0, c, -1).start()
+        each_edge(EDGE_ORDER[low:high], lambda copy: copy.start())
+
+    def start_way(upward, n):
+        way_copy(upward, n).start()
+
+    def pass_way(upward, n):
+        way_copy(upward, n).wait_recv()
+        way_pass(upward, n).start()
 
     map_load.wait()
 
@@ -221,11 +269,12 @@
                 region[c, t, pl.ds(0, PAD), :] = jnp.zeros((PAD, LANES), jnp.float32)
                 region[c, t, pl.ds(region.shape[2] - PAD, PAD), :] = jnp.zeros((PAD, LANES), jnp.float32)
 
-    pl.semaphore_wait(barrier, sectors - 1 + jnp.where(layer > 0, 1, 0) + jnp.where(layer < layers - 1, 1, 0))
+    pl.semaphore_wait(barrier, sectors - 1 + jnp.where(layer > 0, 1, 0) + jnp.where(layer < layers - 1, 1, 0)
+                      + jnp.where(jnp.logical_or(layer == 2, layer == layers - 3), 1, 0))
 
     cavity_shift = shift_copy(two_cavity, 0, tiles, 0, -1)
+    start_blocks(send_r, recv_r, send_r_sem, recv_r_sem, 1)
     cavity_shift.start()
-    start_blocks(send_r, recv_r, send_r_sem, recv_r_sem, 1)
 
     for copy in loads[2 * tiles:]:
         copy.wait()
@@ -239,6 +288,8 @@
                         c, t, pl.ds(PAD + edge, planes, stride=rows), :]
 
     start_edges(0, FIRST)
+    each_way(1, by_way_up, start_way)
+    each_way(0, by_way_down, start_way)
 
     lane = iota(1)
     pieces = []
@@ -346,6 +397,8 @@
     landed_shift = shift_copy(two_landed, tiles, 0, 1, 1)
     landed_shift.start()
     start_edges(SECOND, comps)
+    each_way(1, way_up, pass_way)
+    each_way(0, way_down, pass_way)
 
     def edge_factor(own, got, base, size):
         a, b = ([ref[pl.ds(c * piece + base, size), :] for c in (0, 4)] for ref in (own, got))
@@ -428,15 +481,11 @@
     seam_fix(cavity, cavity_new, mu_c, 0, cavity_ghost)
     landed_shift.wait_send()
 
-    @pl.when(layer < layers - 1)
-    def _():
-        for c in range(comps):
-            edge_copy(1, c, 1).wait_send()
-
-    @pl.when(layer > 0)
-    def _():
-        for c in range(comps):
-            edge_copy(0, c, -1).wait_send()
+    each_edge(EDGE_ORDER, lambda copy: copy.wait_send())
+    each_way(1, by_way_up, lambda upward, n: way_copy(upward, n).wait_send())
+    each_way(0, by_way_down, lambda upward, n: way_copy(upward, n).wait_send())
+    each_way(1, way_up, lambda upward, n: way_pass(upward, n).wait_send())
+    each_way(0, way_down, lambda upward, n: way_pass(upward, n).wait_send())
 
     @pl.when(layer < layers - 1)
     def _():
@@ -493,6 +542,7 @@
             pltpu.SMEM((sectors,), jnp.int32),
             dma((4 * tiles + 2,)), dma((sectors,)), dma((sectors,)), dma((sectors,)), dma((sectors,)),
             dma((2,)), dma((2,)), dma((2, comps)), dma((2, comps)), dma((2,)), dma((2,)),
+            pltpu.VMEM((edge_rows // comps * len(RELAYED), LANES), f32), dma((len(RELAYED),)), dma((len(RELAYED),)),
         ],
         compiler_params=pltpu.CompilerParams(
             collective_id=0, has_side_effects=True, vmem_limit_bytes=24 * 1024 * 1024),

time: 36.5 us -> 35.9 us (0.984)
  the two profiles are of different devices: /device:TPU:33 before, /device:TPU:8 now
where the time goes in v4:
time: 35.9 us; the launch traced here: 35.8 us
  Pallas kernels  34.5 us (96%)
  between operations  1.29 us (4%)
    pallas_call x1, Pallas kernels, shards(): pl.pallas_call(kernel, out_shape=(jax.ShapeDtypeStruct(shape_r, f32), jax...  33.2 us
    pallas_call x1, Pallas kernels, shards(): pl.pallas_call(relay, out_shape=(jax.ShapeDtypeStruct(rotor.shape, f32),...  1.33 us

profile of v4, /device:TPU:8, one launch (start us, length us, event | category | flops | bytes accessed | tf_op | source)
XLA Modules:
  0.0 35.8 jit_solution(6504433375213020294)
XLA Ops:
  1.3 33.2 %shard_map.59 = (f32[5,4,128,128]{3,2,1,0:T(8,128)S(1)}, f32[5,4,64,128]{3,2,1,0:T(8,128)S(1)}) custom-call(s32[32]{0:T(128)} %map_hbm.1, s32[1]{0:T(128)S(6)} %copy.6.offset_ref, f32[5,128,512]{2,1,0:T(8,128)} %bitcast.4, f32[5,64,512]{2,1,0:T(8,128)} %bitcast.5), custom_call_target="tpu_custom_call" | custom-call | tf_op jit(solution)/shard_map/pallas_call | solution.py:528
  34.5 1.3 %shard_map.60 = (f32[5,128,512]{2,1,0:T(8,128)}, f32[5,64,512]{2,1,0:T(8,128)}) custom-call(f32[5,4,128,128]{3,2,1,0:T(8,128)S(1)} %get-tuple-element.6.rotor_in, f32[5,4,64,128]{3,2,1,0:T(8,128)S(1)} %get-tuple-element.7.cavity_in), custom_call_target="tpu_custom_call" | custom-call | tf_op jit(solution)/shard_map/pallas_call | solution.py:551

commit v5 on v4

--- a/solution.py
+++ b/solution.py
@@ -13,7 +13,7 @@
 PAD = 8
 EDGE_ORDER = (0, 4, 1, 2, 3)
 FIRST = 1
-SECOND = 1
+SECOND = 2
 RELAYED = (3,)
 MESH = pl.DeviceIdType.MESH
 

time: 35.9 us -> 35.7 us (level)
  no operation moved by 1% of the time
where the time goes in v5:
time: 35.7 us; the launch traced here: 35.5 us
  Pallas kernels  34.2 us (96%)
  between operations  1.29 us (4%)
    pallas_call x1, Pallas kernels, shards(): pl.pallas_call(kernel, out_shape=(jax.ShapeDtypeStruct(shape_r, f32), jax...  32.9 us
    pallas_call x1, Pallas kernels, shards(): pl.pallas_call(relay, out_shape=(jax.ShapeDtypeStruct(rotor.shape, f32),...  1.33 us

profile of v5, /device:TPU:8, one launch (start us, length us, event | category | flops | bytes accessed | tf_op | source)
XLA Modules:
  0.0 35.5 jit_solution(9432144522718545942)
XLA Ops:
  1.3 32.9 %shard_map.59 = (f32[5,4,128,128]{3,2,1,0:T(8,128)S(1)}, f32[5,4,64,128]{3,2,1,0:T(8,128)S(1)}) custom-call(s32[32]{0:T(128)} %map_hbm.1, s32[1]{0:T(128)S(6)} %copy.6.offset_ref, f32[5,128,512]{2,1,0:T(8,128)} %bitcast.4, f32[5,64,512]{2,1,0:T(8,128)} %bitcast.5), custom_call_target="tpu_custom_call" | custom-call | tf_op jit(solution)/shard_map/pallas_call | solution.py:528
  34.2 1.3 %shard_map.60 = (f32[5,128,512]{2,1,0:T(8,128)}, f32[5,64,512]{2,1,0:T(8,128)}) custom-call(f32[5,4,128,128]{3,2,1,0:T(8,128)S(1)} %get-tuple-element.6.rotor_in, f32[5,4,64,128]{3,2,1,0:T(8,128)S(1)} %get-tuple-element.7.cavity_in), custom_call_target="tpu_custom_call" | custom-call | tf_op jit(solution)/shard_map/pallas_call | solution.py:551
